TPU v7x, 32 devices: a whole 2x2x4 slice. The times are simulated.
32 devices in a mesh: blk: 8 (over z, x), uly: 4 (over y, core).
Axes of the slice: x: 2, y: 2, z: 4, core: 2. Of those that a mesh axis runs over, the one named last changes fastest.
Arguments:
- query_projection: bfloat16 [4096, 4096], P(('blk', 'uly')), may hold values from -4.5 to 4.5
- key_projection: bfloat16 [4096, 512], P(('blk', 'uly')), may hold values from -4.5 to 4.5
- value_projection: bfloat16 [4096, 512], P(('blk', 'uly')), may hold values from -6 to 6
- doc_start: int32 [4096], P('blk'), may hold values from 0 to 4095, as said below
Outputs:
- attn: bfloat16 [4096, 4096], P(('blk', 'uly'))
Inputs may be any that keep to these rules, and one draw needn't show every extreme that they name: Documents are contiguous runs of positions: doc_start[0] = 0, doc_start never falls, doc_start[i] <= i, and doc_start[doc_start[i]] = doc_start[i]. Every document has at most 1024 positions; the first has exactly 1024, and another of exactly 1024 begins strictly inside a block of 512 positions. The last position begins a document of its own.
All inputs are finite; a program needn't handle non-finite values.
Results may differ from a plain program's by a relative error of at most 0.0031.
Values may be sent and summed in bfloat16 or wider, within the bound.
A program may use at most 64 MiB of HBM per device.

v0:
```python
import jax
import jax.numpy as jnp
from jax import lax
from jax.sharding import PartitionSpec as P

HEAD_WIDTH = 128
CYCLE_STEPS = 2
POSITION_GROUP = 512
masked_score = -1e30


def from_behind(block, axis, distance):
    devices = range(lax.axis_size(axis))
    route = [(i - distance, i) for i in devices if i - distance in devices]
    return lax.ppermute(block, axis, route)


def local(query_projection, key_projection, value_projection, doc_start):
    width = lax.axis_size("uly")
    tokens_dev = query_projection.shape[0]
    kv_heads = key_projection.shape[1] // HEAD_WIDTH
    repeats = max(1, width // kv_heads)

    def widen_heads(source):
        split_heads = source.reshape(tokens_dev, kv_heads, 1, HEAD_WIDTH)
        copies = jnp.broadcast_to(split_heads, (tokens_dev, kv_heads, repeats, HEAD_WIDTH))
        return copies.reshape(tokens_dev, kv_heads * repeats * HEAD_WIDTH)

    query_rows = lax.all_to_all(query_projection, "uly", split_axis=1, concat_axis=0, tiled=True)
    key_rows, value_rows = (
        lax.all_to_all(widen_heads(key_projection), "uly", split_axis=1, concat_axis=0, tiled=True),
        lax.all_to_all(
            widen_heads(value_projection), "uly", split_axis=1, concat_axis=0, tiled=True
        ),
    )
    row_count = query_rows.shape[0]
    local_kv = key_rows.shape[1] // HEAD_WIDTH
    local_q = query_rows.shape[1] // HEAD_WIDTH
    query_group_width = local_q // local_kv
    earlier = []
    for step in range(CYCLE_STEPS):
        earlier.insert(0, from_behind((key_rows, value_rows), "blk", step + 1))
    joined_keys = jnp.concatenate([piece[0] for piece in earlier] + [key_rows], axis=0).reshape(
        -1, local_kv, HEAD_WIDTH
    )
    joined_values = jnp.concatenate([piece[1] for piece in earlier] + [value_rows], axis=0).reshape(
        -1, local_kv, HEAD_WIDTH
    )
    lead = CYCLE_STEPS * row_count
    base = lax.axis_index("blk") * row_count
    anchor = base - lead
    query_heads = query_rows.reshape(row_count, local_kv, query_group_width, HEAD_WIDTH)
    score_scale = HEAD_WIDTH ** (-0.5)

    def one_tile(index):
        start = index * POSITION_GROUP
        query_tile = lax.dynamic_slice_in_dim(query_heads, start, POSITION_GROUP, 0)
        starts = lax.dynamic_slice_in_dim(doc_start, start, POSITION_GROUP, 0)
        query_places = base + start + jnp.arange(POSITION_GROUP, dtype=jnp.int32)
        first_tile = (jnp.min(starts) - anchor) // POSITION_GROUP
        last_tile = (lead + start) // POSITION_GROUP

        def add_tile(tile, carry):
            running_maximum, running_sum, running_output = carry
            key_start = tile * POSITION_GROUP
            key_tile = lax.dynamic_slice_in_dim(joined_keys, key_start, POSITION_GROUP, 0)
            value_tile = lax.dynamic_slice_in_dim(joined_values, key_start, POSITION_GROUP, 0)
            key_places = anchor + key_start + jnp.arange(POSITION_GROUP, dtype=jnp.int32)
            seen = (key_places[None, :] >= starts[:, None]) & (
                key_places[None, :] <= query_places[:, None]
            )
            seen = seen[:, None, None, :]
            scores = (
                jnp.einsum(
                    "tkgd,nkd->tkgn", query_tile, key_tile, preferred_element_type=jnp.float32
                )
                * score_scale
            )
            masked = jnp.where(seen, scores, masked_score)
            fresh = jnp.maximum(running_maximum, jnp.max(masked, axis=-1))
            factor = jnp.exp(running_maximum - fresh)
            exps = jnp.where(seen, jnp.exp(masked - fresh[..., None]), 0.0)
            running_sum = running_sum * factor + jnp.sum(exps, axis=-1)
            blended = jnp.einsum(
                "tkgn,nkd->tkgd",
                exps.astype(jnp.bfloat16),
                value_tile,
                preferred_element_type=jnp.float32,
            )
            running_output = running_output * factor[..., None] + blended
            return (fresh, running_sum, running_output)

        running_maximum = jnp.full(
            (POSITION_GROUP, local_kv, query_group_width), masked_score, jnp.float32
        )
        running_sum = jnp.zeros((POSITION_GROUP, local_kv, query_group_width), jnp.float32)
        running_output = jnp.zeros(
            (POSITION_GROUP, local_kv, query_group_width, HEAD_WIDTH), jnp.float32
        )
        running_maximum, running_sum, running_output = lax.fori_loop(
            first_tile, last_tile + 1, add_tile, (running_maximum, running_sum, running_output)
        )
        return (running_output / running_sum[..., None]).astype(jnp.bfloat16)

    outputs = lax.map(one_tile, jnp.arange(row_count // POSITION_GROUP, dtype=jnp.int32))
    attn = outputs.reshape(row_count, local_q * HEAD_WIDTH)
    return lax.all_to_all(attn, "uly", split_axis=0, concat_axis=1, tiled=True)


def solution(mesh):
    placed = (P(("blk", "uly"), None), P(("blk", "uly"), None), P(("blk", "uly"), None), P("blk"))
    return jax.shard_map(
        local, mesh=mesh, in_specs=placed, out_specs=P(("blk", "uly"), None), check_vma=False
    )
```

profile of v0, /device:TPU:18, one launch (start us, length us, event | category | flops | bytes accessed | tf_op | source)
XLA Modules:
  0.0 90.7 jit_solution(1253593889368224903)
XLA Ops:
  0.0 1.7 %copy.24 = bf16[128,512]{0,1:T(8,128)(2,1)} copy(bf16[128,512]{1,0:T(8,128)(2,1)} %param.8) | data formatting | bytes 262144 | tf_op args[2]
  1.7 3.3 %all-to-all-start.2 = ((bf16[128,4,128]{0,2,1:T(8,128)(2,1)}), bf16[128,4,128]{0,2,1:T(8,128)(2,1)S(1)}, u32[]{:S(2)}, u32[]{:S(2)}) async-start(bf16[128,4,128]{0,2,1:T(8,128)(2,1)} %bitcast.5), calls=%async_computation.2 | async-start | bytes 262144 | tf_op jit(solution)/shard_map/all_to_all | solution.py:32
  5.7 3.9 %all-to-all-done.2 = bf16[128,4,128]{0,2,1:T(8,128)(2,1)S(1)} async-done(((bf16[128,4,128]{0,2,1:T(8,128)(2,1)}), bf16[128,4,128]{0,2,1:T(8,128)(2,1)S(1)}, u32[]{:S(2)}, u32[]{:S(2)}) %all-to-all-start.2) | async-done | bytes 131104 | tf_op jit(solution)/shard_map/all_to_all | solution.py:32
  9.6 3.3 %all-to-all-start = ((bf16[128,4,128]{2,0,1:T(8,128)(2,1)}), bf16[128,4,128]{2,0,1:T(8,128)(2,1)S(1)}, u32[]{:S(2)}, u32[]{:S(2)}) async-start(bf16[128,4,128]{2,0,1:T(8,128)(2,1)} %copy_bitcast_fusion.1), calls=%async_computation | async-start | bytes 262144 | tf_op jit(solution)/shard_map/all_to_all | solution.py:31
  12.9 2.3 %copy.39 = bf16[16,4,8,1024]{3,2,0,1:T(8,128)(2,1)} copy(bf16[16,4,8,1024]{3,2,1,0:T(8,128)(2,1)} %bitcast.111) | data formatting | bytes 2097152 | tf_op jit(solution)/shard_map/all_to_all | solution.py:29
  15.2 2.3 %all-to-all-done = bf16[128,4,128]{2,0,1:T(8,128)(2,1)S(1)} async-done(((bf16[128,4,128]{2,0,1:T(8,128)(2,1)}), bf16[128,4,128]{2,0,1:T(8,128)(2,1)S(1)}, u32[]{:S(2)}, u32[]{:S(2)}) %all-to-all-start) | async-done | bytes 131104 | tf_op jit(solution)/shard_map/all_to_all | solution.py:31
  17.5 3.5 %all-to-all-start.1 = ((bf16[128,4,1024]{2,0,1:T(8,128)(2,1)}), bf16[128,4,1024]{2,0,1:T(8,128)(2,1)S(1)}, u32[]{:S(2)}, u32[]{:S(2)}) async-start(bf16[128,4,1024]{2,0,1:T(8,128)(2,1)} %bitcast.83), calls=%async_computation.1 | async-start | bytes 2097152 | tf_op jit(solution)/shard_map/all_to_all | solution.py:29
  21.2 3.5 %collective-permute-start.2 = (bf16[512,128]{1,0:T(8,128)(2,1)S(1)}, bf16[512,128]{1,0:T(8,128)(2,1)S(1)}, u32[]{:S(2)}, u32[]{:S(2)}) collective-permute-start(bf16[512,128]{1,0:T(8,128)(2,1)S(1)} %bitcast.116), channel_id=1, source_target_pairs={{0,8},{4,12},{8,16},{12,20},{16,24},{20,28},{1,9},{5,13},{9,17},{1... | collective-permute-start | bytes 393224 | tf_op jit(solution)/shard_map/ppermute | solution.py:15
  24.7 1.9 %collective-permute-start.3 = (bf16[512,128]{1,0:T(8,128)(2,1)S(1)}, bf16[512,128]{1,0:T(8,128)(2,1)S(1)}, u32[]{:S(2)}, u32[]{:S(2)}) collective-permute-start(bf16[512,128]{1,0:T(8,128)(2,1)S(1)} %bitcast.117), channel_id=1, source_target_pairs={{0,4},{4,8},{8,12},{12,16},{16,20},{20,24},{24,28},{1,5},{5,9},{9,... | collective-permute-start | bytes 393224 | tf_op jit(solution)/shard_map/ppermute | solution.py:15
  28.7 1.9 %collective-permute-start = (bf16[512,128]{1,0:T(8,128)(2,1)S(1)}, bf16[512,128]{1,0:T(8,128)(2,1)S(1)}, u32[]{:S(2)}, u32[]{:S(2)}) collective-permute-start(bf16[512,128]{1,0:T(8,128)(2,1)S(1)} %bitcast.113), channel_id=1, source_target_pairs={{0,8},{4,12},{8,16},{12,20},{16,24},{20,28},{1,9},{5,13},{9,17},{1... | collective-permute-start | bytes 393224 | tf_op jit(solution)/shard_map/ppermute | solution.py:15
  30.6 2.1 %collective-permute-start.1 = (bf16[512,128]{1,0:T(8,128)(2,1)S(1)}, bf16[512,128]{1,0:T(8,128)(2,1)S(1)}, u32[]{:S(2)}, u32[]{:S(2)}) collective-permute-start(bf16[512,128]{1,0:T(8,128)(2,1)S(1)} %bitcast.114), channel_id=1, source_target_pairs={{0,4},{4,8},{8,12},{12,16},{16,20},{20,24},{24,28},{1,5},{5,9},{9,... | collective-permute-start | bytes 393224 | tf_op jit(solution)/shard_map/ppermute | solution.py:15
  33.5 2.6 %collective-permute-done = bf16[512,128]{1,0:T(8,128)(2,1)S(1)} collective-permute-done((bf16[512,128]{1,0:T(8,128)(2,1)S(1)}, bf16[512,128]{1,0:T(8,128)(2,1)S(1)}, u32[]{:S(2)}, u32[]{:S(2)}) %collective-permute-start) | collective-permute-done | bytes 131104 | tf_op jit(solution)/shard_map/ppermute | solution.py:15
  36.2 1.9 %collective-permute-done.1 = bf16[512,128]{1,0:T(8,128)(2,1)S(1)} collective-permute-done((bf16[512,128]{1,0:T(8,128)(2,1)S(1)}, bf16[512,128]{1,0:T(8,128)(2,1)S(1)}, u32[]{:S(2)}, u32[]{:S(2)}) %collective-permute-start.1) | collective-permute-done | bytes 131104 | tf_op jit(solution)/shard_map/ppermute | solution.py:15
  40.2 29.5 %while.24 = (s32[]{:T(128)}, f32[512,1,8]{0,2,1:T(8,128)S(1)}, f32[512,1,8]{0,2,1:T(8,128)}, f32[512,1,8,128]{0,3,2,1:T(8,128)S(1)}, s32[]{:T(128)}, /*index=5*/...) while((s32[]{:T(128)}, f32[512,1,8]{0,2,1:T(8,128)S(1)}, ...), condition=%wide.region_4.5_spmd.clone, body=%wide.region_1.4_spmd.clone.sunk | while | flops 1102853120 | bytes 32123144 | solution.py:100
  41.1 2.4 %fusion.31 = (f32[512,8]{0,1:T(8,128)S(1)}, f32[512,512,8]{1,0,2:T(8,128)S(1)}) fusion(pred[512,512]{0,1:T(8,128)(4,1)S(1)} %compare_and_fusion.2, bf16[512,1,8,128]{3,0,2,1:T(8,128)(2,1)S(1)} %get-tuple-element.297, bf16[1536,1,128]{2,0,1:T(8,128)(2,1)} %get-tuple-element.296, s32[]{:T(128)S(6)} %select_n.64), kind=kOutput, calls=%fused_computation.3.clone.1 | convolution fusion | flops 543158272 | bytes 9846788 | tf_op jit(solution)/shard_map/while/body/eval_jaxpr/while/body/tkgd,nkd->tkgn/dot_general | solution.py:74
  43.6 3.7 %bitcast_add_fusion.5 = f32[512,1,8,128]{0,3,2,1:T(8,128)S(1)} fusion(f32[512,1,8,128]{0,3,2,1:T(8,128)S(1)} %get-tuple-element.279, f32[512,512,8]{1,0,2:T(8,128)S(1)} %get-tuple-element.260, f32[512,8]{0,1:T(8,128)S(1)} %bitcast.106, pred[512,512]{0,1:T(8,128)(4,1)S(1)} %compare_and_fusion.2, f32[512,8]{0,1:T(8,128)S(1)} %get-tuple-element.261, ...), kind=kOutput, calls=%fused_computation.9.clone.1 | convolution fusion | flops 548405248 | bytes 13008900 | tf_op jit(solution)/shard_map/while/body/eval_jaxpr/while/body/tkgn,nkd->tkgd/dot_general | solution.py:84
  47.3 2.0 %fusion.33 = f32[512,8]{0,1:T(8,128)S(1)} fusion(f32[512,512,8]{1,0,2:T(8,128)S(1)} %get-tuple-element.260, f32[512,8]{0,1:T(8,128)S(1)} %bitcast.107, pred[512,512]{0,1:T(8,128)(4,1)S(1)} %compare_and_fusion.2), kind=kLoop, calls=%fused_computation.5.clone.1 | loop fusion | flops 10481664 | bytes 8683520 | tf_op jit(solution)/shard_map/while/body/eval_jaxpr/while/body/reduce_sum | solution.py:83
  51.0 2.4 %fusion.31 = (f32[512,8]{0,1:T(8,128)S(1)}, f32[512,512,8]{1,0,2:T(8,128)S(1)}) fusion(pred[512,512]{0,1:T(8,128)(4,1)S(1)} %compare_and_fusion.2, bf16[512,1,8,128]{3,0,2,1:T(8,128)(2,1)S(1)} %get-tuple-element.297, bf16[1536,1,128]{2,0,1:T(8,128)(2,1)} %get-tuple-element.296, s32[]{:T(128)S(6)} %select_n.64), kind=kOutput, calls=%fused_computation.3.clone.1 | convolution fusion | flops 543158272 | bytes 9846788 | tf_op jit(solution)/shard_map/while/body/eval_jaxpr/while/body/tkgd,nkd->tkgn/dot_general | solution.py:74
  53.4 3.7 %bitcast_add_fusion.5 = f32[512,1,8,128]{0,3,2,1:T(8,128)S(1)} fusion(f32[512,1,8,128]{0,3,2,1:T(8,128)S(1)} %get-tuple-element.279, f32[512,512,8]{1,0,2:T(8,128)S(1)} %get-tuple-element.260, f32[512,8]{0,1:T(8,128)S(1)} %bitcast.106, pred[512,512]{0,1:T(8,128)(4,1)S(1)} %compare_and_fusion.2, f32[512,8]{0,1:T(8,128)S(1)} %get-tuple-element.261, ...), kind=kOutput, calls=%fused_computation.9.clone.1 | convolution fusion | flops 548405248 | bytes 13008900 | tf_op jit(solution)/shard_map/while/body/eval_jaxpr/while/body/tkgn,nkd->tkgd/dot_general | solution.py:84
  57.1 2.0 %fusion.33 = f32[512,8]{0,1:T(8,128)S(1)} fusion(f32[512,512,8]{1,0,2:T(8,128)S(1)} %get-tuple-element.260, f32[512,8]{0,1:T(8,128)S(1)} %bitcast.107, pred[512,512]{0,1:T(8,128)(4,1)S(1)} %compare_and_fusion.2), kind=kLoop, calls=%fused_computation.5.clone.1 | loop fusion | flops 10481664 | bytes 8683520 | tf_op jit(solution)/shard_map/while/body/eval_jaxpr/while/body/reduce_sum | solution.py:83
  60.8 2.4 %fusion.31 = (f32[512,8]{0,1:T(8,128)S(1)}, f32[512,512,8]{1,0,2:T(8,128)S(1)}) fusion(pred[512,512]{0,1:T(8,128)(4,1)S(1)} %compare_and_fusion.2, bf16[512,1,8,128]{3,0,2,1:T(8,128)(2,1)S(1)} %get-tuple-element.297, bf16[1536,1,128]{2,0,1:T(8,128)(2,1)} %get-tuple-element.296, s32[]{:T(128)S(6)} %select_n.64), kind=kOutput, calls=%fused_computation.3.clone.1 | convolution fusion | flops 543158272 | bytes 9846788 | tf_op jit(solution)/shard_map/while/body/eval_jaxpr/while/body/tkgd,nkd->tkgn/dot_general | solution.py:74
  63.2 3.7 %bitcast_add_fusion.5 = f32[512,1,8,128]{0,3,2,1:T(8,128)S(1)} fusion(f32[512,1,8,128]{0,3,2,1:T(8,128)S(1)} %get-tuple-element.279, f32[512,512,8]{1,0,2:T(8,128)S(1)} %get-tuple-element.260, f32[512,8]{0,1:T(8,128)S(1)} %bitcast.106, pred[512,512]{0,1:T(8,128)(4,1)S(1)} %compare_and_fusion.2, f32[512,8]{0,1:T(8,128)S(1)} %get-tuple-element.261, ...), kind=kOutput, calls=%fused_computation.9.clone.1 | convolution fusion | flops 548405248 | bytes 13008900 | tf_op jit(solution)/shard_map/while/body/eval_jaxpr/while/body/tkgn,nkd->tkgd/dot_general | solution.py:84
  67.0 2.0 %fusion.33 = f32[512,8]{0,1:T(8,128)S(1)} fusion(f32[512,512,8]{1,0,2:T(8,128)S(1)} %get-tuple-element.260, f32[512,8]{0,1:T(8,128)S(1)} %bitcast.107, pred[512,512]{0,1:T(8,128)(4,1)S(1)} %compare_and_fusion.2), kind=kLoop, calls=%fused_computation.5.clone.1 | loop fusion | flops 10481664 | bytes 8683520 | tf_op jit(solution)/shard_map/while/body/eval_jaxpr/while/body/reduce_sum | solution.py:83
  71.6 17.1 %all_to_all.73 = bf16[4,128,1024]{2,1,0:T(8,128)(2,1)S(1)} all-to-all(bf16[4,128,1024]{2,1,0:T(8,128)(2,1)S(1)} %copy.32), channel_id=1, replica_groups=mesh['blk'=8,'uly'=4] {'uly'}, dimensions={0} | all-to-all | bytes 2097152 | tf_op jit(solution)/shard_map/all_to_all | solution.py:107
  (47 shorter events, 13.7 us)
Async XLA Ops:
  0.0 5.0 %copy-start = (bf16[128,512]{1,0:T(8,128)(2,1)S(1)}, bf16[128,512]{1,0:T(8,128)(2,1)}, u32[]{:S(2)}) copy-start(bf16[128,512]{1,0:T(8,128)(2,1)} %param.7) | copy-start | bytes 393220
  1.7 7.9 %all-to-all-start.2 = ((bf16[128,4,128]{0,2,1:T(8,128)(2,1)}), bf16[128,4,128]{0,2,1:T(8,128)(2,1)S(1)}, u32[]{:S(2)}, u32[]{:S(2)}) async-start(bf16[128,4,128]{0,2,1:T(8,128)(2,1)} %bitcast.5), calls=%async_computation.2 | async-start | bytes 262144 | tf_op jit(solution)/shard_map/all_to_all | solution.py:32
  9.6 7.9 %all-to-all-start = ((bf16[128,4,128]{2,0,1:T(8,128)(2,1)}), bf16[128,4,128]{2,0,1:T(8,128)(2,1)S(1)}, u32[]{:S(2)}, u32[]{:S(2)}) async-start(bf16[128,4,128]{2,0,1:T(8,128)(2,1)} %copy_bitcast_fusion.1), calls=%async_computation | async-start | bytes 262144 | tf_op jit(solution)/shard_map/all_to_all | solution.py:31
  17.5 21.4 %all-to-all-start.1 = ((bf16[128,4,1024]{2,0,1:T(8,128)(2,1)}), bf16[128,4,1024]{2,0,1:T(8,128)(2,1)S(1)}, u32[]{:S(2)}, u32[]{:S(2)}) async-start(bf16[128,4,1024]{2,0,1:T(8,128)(2,1)} %bitcast.83), calls=%async_computation.1 | async-start | bytes 2097152 | tf_op jit(solution)/shard_map/all_to_all | solution.py:29
  21.2 11.6 %collective-permute-start.2 = (bf16[512,128]{1,0:T(8,128)(2,1)S(1)}, bf16[512,128]{1,0:T(8,128)(2,1)S(1)}, u32[]{:S(2)}, u32[]{:S(2)}) collective-permute-start(bf16[512,128]{1,0:T(8,128)(2,1)S(1)} %bitcast.116), channel_id=1, source_target_pairs={{0,8},{4,12},{8,16},{12,20},{16,24},{20,28},{1,9},{5,13},{9,17},{1... | collective-permute-start | bytes 393224 | tf_op jit(solution)/shard_map/ppermute | solution.py:15
  24.7 8.1 %collective-permute-start.3 = (bf16[512,128]{1,0:T(8,128)(2,1)S(1)}, bf16[512,128]{1,0:T(8,128)(2,1)S(1)}, u32[]{:S(2)}, u32[]{:S(2)}) collective-permute-start(bf16[512,128]{1,0:T(8,128)(2,1)S(1)} %bitcast.117), channel_id=1, source_target_pairs={{0,4},{4,8},{8,12},{12,16},{16,20},{20,24},{24,28},{1,5},{5,9},{9,... | collective-permute-start | bytes 393224 | tf_op jit(solution)/shard_map/ppermute | solution.py:15
  28.7 7.5 %collective-permute-start = (bf16[512,128]{1,0:T(8,128)(2,1)S(1)}, bf16[512,128]{1,0:T(8,128)(2,1)S(1)}, u32[]{:S(2)}, u32[]{:S(2)}) collective-permute-start(bf16[512,128]{1,0:T(8,128)(2,1)S(1)} %bitcast.113), channel_id=1, source_target_pairs={{0,8},{4,12},{8,16},{12,20},{16,24},{20,28},{1,9},{5,13},{9,17},{1... | collective-permute-start | bytes 393224 | tf_op jit(solution)/shard_map/ppermute | solution.py:15
  30.6 7.5 %collective-permute-start.1 = (bf16[512,128]{1,0:T(8,128)(2,1)S(1)}, bf16[512,128]{1,0:T(8,128)(2,1)S(1)}, u32[]{:S(2)}, u32[]{:S(2)}) collective-permute-start(bf16[512,128]{1,0:T(8,128)(2,1)S(1)} %bitcast.114), channel_id=1, source_target_pairs={{0,4},{4,8},{8,12},{12,16},{16,20},{20,24},{24,28},{1,5},{5,9},{9,... | collective-permute-start | bytes 393224 | tf_op jit(solution)/shard_map/ppermute | solution.py:15
  43.6 5.8 %copy-start.1 = (f32[512,1,8]{0,2,1:T(8,128)S(1)}, f32[512,1,8]{0,2,1:T(8,128)}, u32[]{:S(2)}) copy-start(f32[512,1,8]{0,2,1:T(8,128)} %get-tuple-element.278) | copy-start | bytes 49156 | tf_op jit(solution)/shard_map/while/body/eval_jaxpr/while
  49.4 0.6 copy-start.2
  53.4 5.8 %copy-start.1 = (f32[512,1,8]{0,2,1:T(8,128)S(1)}, f32[512,1,8]{0,2,1:T(8,128)}, u32[]{:S(2)}) copy-start(f32[512,1,8]{0,2,1:T(8,128)} %get-tuple-element.278) | copy-start | bytes 49156 | tf_op jit(solution)/shard_map/while/body/eval_jaxpr/while
  59.2 0.6 copy-start.2
  63.2 5.8 %copy-start.1 = (f32[512,1,8]{0,2,1:T(8,128)S(1)}, f32[512,1,8]{0,2,1:T(8,128)}, u32[]{:S(2)}) copy-start(f32[512,1,8]{0,2,1:T(8,128)} %get-tuple-element.278) | copy-start | bytes 49156 | tf_op jit(solution)/shard_map/while/body/eval_jaxpr/while
  69.0 0.6 copy-start.2
where the time goes:
time: 91.6 us; the launch traced here: 90.7 us
  starting transfers between devices  19.6 us (21%)
  matrix products  18.4 us (20%)
  blocking collectives  17.1 us (19%)
  other arithmetic  13 us (14%)
  local copies, waits for them, and re-layouts  10.8 us (12%)
  waiting for transfers between devices  10.7 us (12%)
    all_to_all x1, blocking collectives, local(): return lax.all_to_all(attn, 'uly', split_axis=0, concat_axis=1, tiled=True)  17.1 us
    dot_general x3, matrix products, add_tile(): jnp.einsum('tkgn,nkd->tkgd', exps.astype(jnp.bfloat16), value_tile, prefe...  11.2 us
    ppermute x4, starting transfers between devices, from_behind(): return lax.ppermute(block, axis, route)  9.44 us
    dot_general x3, matrix products, add_tile(): jnp.einsum('tkgd,nkd->tkgn', query_tile, key_tile, preferred_element_type...  7.21 us
    reduce_sum x3, other arithmetic, add_tile(): running_sum = running_sum * factor + jnp.sum(exps, axis=-1)  6.1 us
    ppermute x4, waiting for transfers between devices, from_behind(): return lax.ppermute(block, axis, route)  4.56 us
    all_to_all x1, waiting for transfers between devices, local(): lax.all_to_all(widen_heads(value_projection), 'uly', split_axis=1, concat...  3.88 us
    all_to_all x1, starting transfers between devices, local(): lax.all_to_all(query_projection, 'uly', split_axis=1, concat_axis=0, tile...  3.52 us
  transfers between devices with their start and end apart: 7, of which 4 were waited for; matrix products, arithmetic and copies ran while one was open for 7% of the time, Pallas kernels for 0%

commit v1 on v0

--- a/solution.py
+++ b/solution.py
@@ -7,6 +7,29 @@
 CYCLE_STEPS = 2
 POSITION_GROUP = 512
 masked_score = -1e30
+
+
+def split_up(value, dim, count):
+    before, after = (value.shape[:dim], value.shape[dim + 1 :])
+    return jnp.moveaxis(value.reshape(*before, count, -1, *after), dim, 0)
+
+
+def joined_along(pieces, dim):
+    pieces = jnp.moveaxis(pieces, 0, dim)
+    lengths = pieces.shape
+    return pieces.reshape(*lengths[:dim], lengths[dim] * lengths[dim + 1], *lengths[dim + 2 :])
+
+
+def rotated_exchange(value, axis, split_dim, concat_dim):
+    size, index = (lax.axis_size(axis), lax.axis_index(axis))
+    parts = split_up(value, split_dim, size)
+    result = parts
+    for step in range(1, size):
+        target, source = ((index + step) % size, (index - step) % size)
+        sent = lax.dynamic_index_in_dim(parts, target, 0)
+        other = lax.ppermute(sent, axis, [(i, (i + step) % size) for i in range(size)])
+        result = lax.dynamic_update_slice_in_dim(result, other, source, axis=0)
+    return joined_along(result, concat_dim)
 
 
 def from_behind(block, axis, distance):
@@ -28,7 +51,7 @@
 
     query_rows = lax.all_to_all(query_projection, "uly", split_axis=1, concat_axis=0, tiled=True)
     key_rows, value_rows = (
-        lax.all_to_all(widen_heads(key_projection), "uly", split_axis=1, concat_axis=0, tiled=True),
+        rotated_exchange(widen_heads(key_projection), "uly", 1, 0),
         lax.all_to_all(
             widen_heads(value_projection), "uly", split_axis=1, concat_axis=0, tiled=True
         ),

time: 91.6 us -> 82.6 us (0.902)
  waiting for transfers between devices: 10.7 us -> 6.78 us
  other arithmetic: 13 us -> 10.2 us
  local copies, waits for them, and re-layouts: 10.8 us -> 8.89 us
    all_to_all x1 -> x0, starting transfers between devices: 3.32 us -> none  [local(): lax.all_to_all(widen_heads(key_projection), 'uly', split_axis=1, concat_a...]
    ppermute x0 -> x3, starting transfers between devices: none -> 3.03 us  [rotated_exchange(): lax.ppermute(sent, axis, [(i, (i + step) % size) for i in range(size)])]
    all_to_all x1 -> x0, waiting for transfers between devices: 2.28 us -> none  [local(): lax.all_to_all(widen_heads(key_projection), 'uly', split_axis=1, concat_a...]
    and x3, other arithmetic: 2.85 us -> 0.81 us  [add_tile(): (key_places[None, :] >= starts[:, None]) & (key_places[None, :] <= query_...]
    while x15 -> x3, local copies, waits for them, and re-layouts: 1.83 us -> 0.01 us
    all_to_all x1, waiting for transfers between devices: 3.88 us -> 2.21 us  [local(): lax.all_to_all(widen_heads(value_projection), 'uly', split_axis=1, concat...]
    unnamed x5 -> x6, local copies, waits for them, and re-layouts: 2.11 us -> 3.1 us
  transfers between devices with their start and end apart: 7 -> 9, of which waited for: 4 -> 3; matrix products, arithmetic and copies ran while one was open for 7% -> 9% of each run, Pallas kernels for 0% -> 0%
where the time goes in v1:
time: 82.6 us; the launch traced here: 82 us
  starting transfers between devices  19.3 us (23%)
  matrix products  18.4 us (22%)
  blocking collectives  17.1 us (21%)
  other arithmetic  10.2 us (12%)
  local copies, waits for them, and re-layouts  8.89 us (11%)
  waiting for transfers between devices  6.78 us (8%)
  between operations  1.01 us (1%)
    all_to_all x1, blocking collectives, local(): return lax.all_to_all(attn, 'uly', split_axis=0, concat_axis=1, tiled=True)  17.1 us
    dot_general x3, matrix products, add_tile(): jnp.einsum('tkgn,nkd->tkgd', exps.astype(jnp.bfloat16), value_tile, prefe...  11.2 us
    ppermute x4, starting transfers between devices, from_behind(): return lax.ppermute(block, axis, route)  9.44 us
    dot_general x3, matrix products, add_tile(): jnp.einsum('tkgd,nkd->tkgn', query_tile, key_tile, preferred_element_type...  7.21 us
    reduce_sum x3, other arithmetic, add_tile(): running_sum = running_sum * factor + jnp.sum(exps, axis=-1)  6.1 us
    ppermute x4, waiting for transfers between devices, from_behind(): return lax.ppermute(block, axis, route)  4.56 us
    all_to_all x1, starting transfers between devices, local(): lax.all_to_all(query_projection, 'uly', split_axis=1, concat_axis=0, tile...  3.52 us
    all_to_all x1, starting transfers between devices, local(): lax.all_to_all(widen_heads(value_projection), 'uly', split_axis=1, concat...  3.32 us
  transfers between devices with their start and end apart: 9, of which 3 were waited for; matrix products, arithmetic and copies ran while one was open for 9% of the time, Pallas kernels for 0%

profile of v1, /device:TPU:18, one launch (start us, length us, event | category | flops | bytes accessed | tf_op | source)
XLA Modules:
  0.0 82.0 jit_solution(11042134039627610143)
XLA Ops:
  1.1 1.6 %collective-permute-start.1 = (bf16[1,128,128]{1,2,0:T(8,128)(2,1)S(1)}, bf16[1,128,128]{1,2,0:T(8,128)(2,1)S(1)}, u32[]{:S(2)}, u32[]{:S(2)}) collective-permute-start(bf16[1,128,128]{1,2,0:T(8,128)(2,1)S(1)} %get-tuple-element.210), channel_id=1, source_target_pairs={{0,2},{1,3},{2,0},{3,1},{4,6},{5,7},{6,4},{7,5},{8,10},{9,11},{10,... | collective-permute-start | bytes 98312 | tf_op jit(solution)/shard_map/ppermute | solution.py:30
  4.1 1.7 %copy.62 = bf16[128,512]{0,1:T(8,128)(2,1)} copy(bf16[128,512]{1,0:T(8,128)(2,1)} %param.8) | data formatting | bytes 262144 | tf_op args[2]
  5.8 3.3 %all-to-all-start.1 = ((bf16[128,4,128]{0,2,1:T(8,128)(2,1)}), bf16[128,4,128]{0,2,1:T(8,128)(2,1)S(1)}, u32[]{:S(2)}, u32[]{:S(2)}) async-start(bf16[128,4,128]{0,2,1:T(8,128)(2,1)} %bitcast.8), calls=%async_computation.1 | async-start | bytes 262144 | tf_op jit(solution)/shard_map/all_to_all | solution.py:55
  9.2 2.3 %copy.78 = bf16[16,4,8,1024]{3,2,0,1:T(8,128)(2,1)} copy(bf16[16,4,8,1024]{3,2,1,0:T(8,128)(2,1)} %bitcast.113) | data formatting | bytes 2097152 | tf_op jit(solution)/shard_map/all_to_all | solution.py:52
  11.5 2.2 %all-to-all-done.1 = bf16[128,4,128]{0,2,1:T(8,128)(2,1)S(1)} async-done(((bf16[128,4,128]{0,2,1:T(8,128)(2,1)}), bf16[128,4,128]{0,2,1:T(8,128)(2,1)S(1)}, u32[]{:S(2)}, u32[]{:S(2)}) %all-to-all-start.1) | async-done | bytes 131104 | tf_op jit(solution)/shard_map/all_to_all | solution.py:55
  13.7 3.5 %all-to-all-start = ((bf16[128,4,1024]{2,0,1:T(8,128)(2,1)}), bf16[128,4,1024]{2,0,1:T(8,128)(2,1)S(1)}, u32[]{:S(2)}, u32[]{:S(2)}) async-start(bf16[128,4,1024]{2,0,1:T(8,128)(2,1)} %bitcast.85), calls=%async_computation | async-start | bytes 2097152 | tf_op jit(solution)/shard_map/all_to_all | solution.py:52
  17.4 3.5 %collective-permute-start.3 = (bf16[512,128]{1,0:T(8,128)(2,1)S(1)}, bf16[512,128]{1,0:T(8,128)(2,1)S(1)}, u32[]{:S(2)}, u32[]{:S(2)}) collective-permute-start(bf16[512,128]{1,0:T(8,128)(2,1)S(1)} %bitcast.117), channel_id=1, source_target_pairs={{0,8},{4,12},{8,16},{12,20},{16,24},{20,28},{1,9},{5,13},{9,17},{1... | collective-permute-start | bytes 393224 | tf_op jit(solution)/shard_map/ppermute | solution.py:38
  20.9 1.9 %collective-permute-start.4 = (bf16[512,128]{1,0:T(8,128)(2,1)S(1)}, bf16[512,128]{1,0:T(8,128)(2,1)S(1)}, u32[]{:S(2)}, u32[]{:S(2)}) collective-permute-start(bf16[512,128]{1,0:T(8,128)(2,1)S(1)} %bitcast.118), channel_id=1, source_target_pairs={{0,4},{4,8},{8,12},{12,16},{16,20},{20,24},{24,28},{1,5},{5,9},{9,... | collective-permute-start | bytes 393224 | tf_op jit(solution)/shard_map/ppermute | solution.py:38
  22.8 1.4 %reduce_min.10 = s32[]{:T(128)} reduce(s32[512]{0:T(512)} %param.9, s32[]{:T(128)} %constant.139.clone.1), dimensions={0}, to_apply=%region_0.1 | reduce | flops 511 | bytes 2056 | tf_op jit(solution)/shard_map/while/body/eval_jaxpr/reduce_min | solution.py:83
  25.1 1.9 %collective-permute-start.5 = (bf16[512,128]{1,0:T(8,128)(2,1)S(1)}, bf16[512,128]{1,0:T(8,128)(2,1)S(1)}, u32[]{:S(2)}, u32[]{:S(2)}) collective-permute-start(bf16[512,128]{1,0:T(8,128)(2,1)S(1)} %bitcast.120), channel_id=1, source_target_pairs={{0,8},{4,12},{8,16},{12,20},{16,24},{20,28},{1,9},{5,13},{9,17},{1... | collective-permute-start | bytes 393224 | tf_op jit(solution)/shard_map/ppermute | solution.py:38
  27.0 2.1 %collective-permute-start.6 = (bf16[512,128]{1,0:T(8,128)(2,1)S(1)}, bf16[512,128]{1,0:T(8,128)(2,1)S(1)}, u32[]{:S(2)}, u32[]{:S(2)}) collective-permute-start(bf16[512,128]{1,0:T(8,128)(2,1)S(1)} %bitcast.121), channel_id=1, source_target_pairs={{0,4},{4,8},{8,12},{12,16},{16,20},{20,24},{24,28},{1,5},{5,9},{9,... | collective-permute-start | bytes 393224 | tf_op jit(solution)/shard_map/ppermute | solution.py:38
  29.9 2.6 %collective-permute-done.5 = bf16[512,128]{1,0:T(8,128)(2,1)S(1)} collective-permute-done((bf16[512,128]{1,0:T(8,128)(2,1)S(1)}, bf16[512,128]{1,0:T(8,128)(2,1)S(1)}, u32[]{:S(2)}, u32[]{:S(2)}) %collective-permute-start.5) | collective-permute-done | bytes 131104 | tf_op jit(solution)/shard_map/ppermute | solution.py:38
  32.5 1.9 %collective-permute-done.6 = bf16[512,128]{1,0:T(8,128)(2,1)S(1)} collective-permute-done((bf16[512,128]{1,0:T(8,128)(2,1)S(1)}, bf16[512,128]{1,0:T(8,128)(2,1)S(1)}, u32[]{:S(2)}, u32[]{:S(2)}) %collective-permute-start.6) | collective-permute-done | bytes 131104 | tf_op jit(solution)/shard_map/ppermute | solution.py:38
  36.0 25.7 %while.24 = (s32[]{:T(128)}, f32[512,1,8]{0,2,1:T(8,128)S(1)}, f32[512,1,8]{0,2,1:T(8,128)S(1)}, f32[512,1,8,128]{0,3,2,1:T(8,128)S(1)}, s32[]{:T(128)}, /*index...) while((s32[]{:T(128)}, f32[512,1,8]{0,2,1:T(8,128)S(1)}, ...), condition=%wide.region_4.5_spmd.clone, body=%wide.region_1.4_spmd.clone.sunk | while | flops 1102853120 | bytes 31992016 | solution.py:123
  36.3 2.4 %fusion.30 = (f32[512,8]{0,1:T(8,128)S(1)}, f32[512,512,8]{1,0,2:T(8,128)S(1)}) fusion(pred[512,512]{0,1:T(8,128)(4,1)S(1)} %compare_and_fusion.2, bf16[512,1,8,128]{3,0,2,1:T(8,128)(2,1)S(1)} %get-tuple-element.320, bf16[1536,1,128]{2,0,1:T(8,128)(2,1)} %get-tuple-element.319, s32[]{:T(128)S(6)} %select_n.121), kind=kOutput, calls=%fused_computation.3.clone.1 | convolution fusion | flops 543158272 | bytes 9846788 | tf_op jit(solution)/shard_map/while/body/eval_jaxpr/while/body/tkgd,nkd->tkgn/dot_general | solution.py:97
  38.7 3.7 %bitcast_add_fusion.5 = f32[512,1,8,128]{0,3,2,1:T(8,128)S(1)} fusion(f32[512,1,8,128]{0,3,2,1:T(8,128)S(1)} %get-tuple-element.302, f32[512,512,8]{1,0,2:T(8,128)S(1)} %get-tuple-element.283, f32[512,8]{0,1:T(8,128)S(1)} %bitcast.108, pred[512,512]{0,1:T(8,128)(4,1)S(1)} %compare_and_fusion.2, f32[512,8]{0,1:T(8,128)S(1)} %get-tuple-element.284, ...), kind=kOutput, calls=%fused_computation.9.clone.1 | convolution fusion | flops 548405248 | bytes 13008900 | tf_op jit(solution)/shard_map/while/body/eval_jaxpr/while/body/tkgn,nkd->tkgd/dot_general | solution.py:107
  42.4 2.0 %fusion.32 = f32[512,8]{0,1:T(8,128)S(1)} fusion(f32[512,512,8]{1,0,2:T(8,128)S(1)} %get-tuple-element.283, f32[512,8]{0,1:T(8,128)S(1)} %bitcast.109, pred[512,512]{0,1:T(8,128)(4,1)S(1)} %compare_and_fusion.2), kind=kLoop, calls=%fused_computation.5.clone.1 | loop fusion | flops 10481664 | bytes 8683520 | tf_op jit(solution)/shard_map/while/body/eval_jaxpr/while/body/reduce_sum | solution.py:106
  44.8 2.4 %fusion.30 = (f32[512,8]{0,1:T(8,128)S(1)}, f32[512,512,8]{1,0,2:T(8,128)S(1)}) fusion(pred[512,512]{0,1:T(8,128)(4,1)S(1)} %compare_and_fusion.2, bf16[512,1,8,128]{3,0,2,1:T(8,128)(2,1)S(1)} %get-tuple-element.320, bf16[1536,1,128]{2,0,1:T(8,128)(2,1)} %get-tuple-element.319, s32[]{:T(128)S(6)} %select_n.121), kind=kOutput, calls=%fused_computation.3.clone.1 | convolution fusion | flops 543158272 | bytes 9846788 | tf_op jit(solution)/shard_map/while/body/eval_jaxpr/while/body/tkgd,nkd->tkgn/dot_general | solution.py:97
  47.3 3.7 %bitcast_add_fusion.5 = f32[512,1,8,128]{0,3,2,1:T(8,128)S(1)} fusion(f32[512,1,8,128]{0,3,2,1:T(8,128)S(1)} %get-tuple-element.302, f32[512,512,8]{1,0,2:T(8,128)S(1)} %get-tuple-element.283, f32[512,8]{0,1:T(8,128)S(1)} %bitcast.108, pred[512,512]{0,1:T(8,128)(4,1)S(1)} %compare_and_fusion.2, f32[512,8]{0,1:T(8,128)S(1)} %get-tuple-element.284, ...), kind=kOutput, calls=%fused_computation.9.clone.1 | convolution fusion | flops 548405248 | bytes 13008900 | tf_op jit(solution)/shard_map/while/body/eval_jaxpr/while/body/tkgn,nkd->tkgd/dot_general | solution.py:107
  51.0 2.0 %fusion.32 = f32[512,8]{0,1:T(8,128)S(1)} fusion(f32[512,512,8]{1,0,2:T(8,128)S(1)} %get-tuple-element.283, f32[512,8]{0,1:T(8,128)S(1)} %bitcast.109, pred[512,512]{0,1:T(8,128)(4,1)S(1)} %compare_and_fusion.2), kind=kLoop, calls=%fused_computation.5.clone.1 | loop fusion | flops 10481664 | bytes 8683520 | tf_op jit(solution)/shard_map/while/body/eval_jaxpr/while/body/reduce_sum | solution.py:106
  53.4 2.4 %fusion.30 = (f32[512,8]{0,1:T(8,128)S(1)}, f32[512,512,8]{1,0,2:T(8,128)S(1)}) fusion(pred[512,512]{0,1:T(8,128)(4,1)S(1)} %compare_and_fusion.2, bf16[512,1,8,128]{3,0,2,1:T(8,128)(2,1)S(1)} %get-tuple-element.320, bf16[1536,1,128]{2,0,1:T(8,128)(2,1)} %get-tuple-element.319, s32[]{:T(128)S(6)} %select_n.121), kind=kOutput, calls=%fused_computation.3.clone.1 | convolution fusion | flops 543158272 | bytes 9846788 | tf_op jit(solution)/shard_map/while/body/eval_jaxpr/while/body/tkgd,nkd->tkgn/dot_general | solution.py:97
  55.8 3.7 %bitcast_add_fusion.5 = f32[512,1,8,128]{0,3,2,1:T(8,128)S(1)} fusion(f32[512,1,8,128]{0,3,2,1:T(8,128)S(1)} %get-tuple-element.302, f32[512,512,8]{1,0,2:T(8,128)S(1)} %get-tuple-element.283, f32[512,8]{0,1:T(8,128)S(1)} %bitcast.108, pred[512,512]{0,1:T(8,128)(4,1)S(1)} %compare_and_fusion.2, f32[512,8]{0,1:T(8,128)S(1)} %get-tuple-element.284, ...), kind=kOutput, calls=%fused_computation.9.clone.1 | convolution fusion | flops 548405248 | bytes 13008900 | tf_op jit(solution)/shard_map/while/body/eval_jaxpr/while/body/tkgn,nkd->tkgd/dot_general | solution.py:107
  59.6 2.0 %fusion.32 = f32[512,8]{0,1:T(8,128)S(1)} fusion(f32[512,512,8]{1,0,2:T(8,128)S(1)} %get-tuple-element.283, f32[512,8]{0,1:T(8,128)S(1)} %bitcast.109, pred[512,512]{0,1:T(8,128)(4,1)S(1)} %compare_and_fusion.2), kind=kLoop, calls=%fused_computation.5.clone.1 | loop fusion | flops 10481664 | bytes 8683520 | tf_op jit(solution)/shard_map/while/body/eval_jaxpr/while/body/reduce_sum | solution.py:106
  62.9 17.1 %all_to_all.54 = bf16[4,128,1024]{2,1,0:T(8,128)(2,1)S(1)} all-to-all(bf16[4,128,1024]{2,1,0:T(8,128)(2,1)S(1)} %copy.73), channel_id=1, replica_groups=mesh['blk'=8,'uly'=4] {'uly'}, dimensions={0} | all-to-all | bytes 2097152 | tf_op jit(solution)/shard_map/all_to_all | solution.py:130
  (44 shorter events, 9.2 us)
Async XLA Ops:
  0.0 35.9 %copy-start = (s32[512]{0:T(512)S(1)}, s32[512]{0:T(512)}, u32[]{:S(2)}) copy-start(s32[512]{0:T(512)} %param.9) | copy-start | bytes 6148
  1.1 10.4 %collective-permute-start = (bf16[1,128,128]{1,2,0:T(8,128)(2,1)S(1)}, bf16[1,128,128]{1,2,0:T(8,128)(2,1)S(1)}, u32[]{:S(2)}, u32[]{:S(2)}) collective-permute-start(bf16[1,128,128]{1,2,0:T(8,128)(2,1)S(1)} %get-tuple-element.211), channel_id=1, source_target_pairs={{0,1},{1,2},{2,3},{3,0},{4,5},{5,6},{6,7},{7,4},{8,9},{9,10},{10,1... | collective-permute-start | bytes 98312 | tf_op jit(solution)/shard_map/ppermute | solution.py:30
  1.1 16.1 %collective-permute-start.1 = (bf16[1,128,128]{1,2,0:T(8,128)(2,1)S(1)}, bf16[1,128,128]{1,2,0:T(8,128)(2,1)S(1)}, u32[]{:S(2)}, u32[]{:S(2)}) collective-permute-start(bf16[1,128,128]{1,2,0:T(8,128)(2,1)S(1)} %get-tuple-element.210), channel_id=1, source_target_pairs={{0,2},{1,3},{2,0},{3,1},{4,6},{5,7},{6,4},{7,5},{8,10},{9,11},{10,... | collective-permute-start | bytes 98312 | tf_op jit(solution)/shard_map/ppermute | solution.py:30
  2.7 14.5 %collective-permute-start.2 = (bf16[1,128,128]{1,2,0:T(8,128)(2,1)S(1)}, bf16[1,128,128]{1,2,0:T(8,128)(2,1)S(1)}, u32[]{:S(2)}, u32[]{:S(2)}) collective-permute-start(bf16[1,128,128]{1,2,0:T(8,128)(2,1)S(1)} %get-tuple-element.209), channel_id=1, source_target_pairs={{0,3},{1,0},{2,1},{3,2},{4,7},{5,4},{6,5},{7,6},{8,11},{9,8},{10,9... | collective-permute-start | bytes 98312 | tf_op jit(solution)/shard_map/ppermute | solution.py:30
  5.8 7.9 %all-to-all-start.1 = ((bf16[128,4,128]{0,2,1:T(8,128)(2,1)}), bf16[128,4,128]{0,2,1:T(8,128)(2,1)S(1)}, u32[]{:S(2)}, u32[]{:S(2)}) async-start(bf16[128,4,128]{0,2,1:T(8,128)(2,1)} %bitcast.8), calls=%async_computation.1 | async-start | bytes 262144 | tf_op jit(solution)/shard_map/all_to_all | solution.py:55
  13.7 21.6 %all-to-all-start = ((bf16[128,4,1024]{2,0,1:T(8,128)(2,1)}), bf16[128,4,1024]{2,0,1:T(8,128)(2,1)S(1)}, u32[]{:S(2)}, u32[]{:S(2)}) async-start(bf16[128,4,1024]{2,0,1:T(8,128)(2,1)} %bitcast.85), calls=%async_computation | async-start | bytes 2097152 | tf_op jit(solution)/shard_map/all_to_all | solution.py:52
  17.4 11.7 %collective-permute-start.3 = (bf16[512,128]{1,0:T(8,128)(2,1)S(1)}, bf16[512,128]{1,0:T(8,128)(2,1)S(1)}, u32[]{:S(2)}, u32[]{:S(2)}) collective-permute-start(bf16[512,128]{1,0:T(8,128)(2,1)S(1)} %bitcast.117), channel_id=1, source_target_pairs={{0,8},{4,12},{8,16},{12,20},{16,24},{20,28},{1,9},{5,13},{9,17},{1... | collective-permute-start | bytes 393224 | tf_op jit(solution)/shard_map/ppermute | solution.py:38
  20.9 8.2 %collective-permute-start.4 = (bf16[512,128]{1,0:T(8,128)(2,1)S(1)}, bf16[512,128]{1,0:T(8,128)(2,1)S(1)}, u32[]{:S(2)}, u32[]{:S(2)}) collective-permute-start(bf16[512,128]{1,0:T(8,128)(2,1)S(1)} %bitcast.118), channel_id=1, source_target_pairs={{0,4},{4,8},{8,12},{12,16},{16,20},{20,24},{24,28},{1,5},{5,9},{9,... | collective-permute-start | bytes 393224 | tf_op jit(solution)/shard_map/ppermute | solution.py:38
  25.1 7.5 %collective-permute-start.5 = (bf16[512,128]{1,0:T(8,128)(2,1)S(1)}, bf16[512,128]{1,0:T(8,128)(2,1)S(1)}, u32[]{:S(2)}, u32[]{:S(2)}) collective-permute-start(bf16[512,128]{1,0:T(8,128)(2,1)S(1)} %bitcast.120), channel_id=1, source_target_pairs={{0,8},{4,12},{8,16},{12,20},{16,24},{20,28},{1,9},{5,13},{9,17},{1... | collective-permute-start | bytes 393224 | tf_op jit(solution)/shard_map/ppermute | solution.py:38
  27.0 7.5 %collective-permute-start.6 = (bf16[512,128]{1,0:T(8,128)(2,1)S(1)}, bf16[512,128]{1,0:T(8,128)(2,1)S(1)}, u32[]{:S(2)}, u32[]{:S(2)}) collective-permute-start(bf16[512,128]{1,0:T(8,128)(2,1)S(1)} %bitcast.121), channel_id=1, source_target_pairs={{0,4},{4,8},{8,12},{12,16},{16,20},{20,24},{24,28},{1,5},{5,9},{9,... | collective-permute-start | bytes 393224 | tf_op jit(solution)/shard_map/ppermute | solution.py:38
